TPU v7x, 32 devices: a whole 2x2x4 slice. The times are simulated.
32 devices in a mesh: obj: 4 (over z), plane: 4 (over y, core), tile: 2 (over x).
Axes of the slice: x: 2, y: 2, z: 4, core: 2. Of those that a mesh axis runs over, the one named last changes fastest.
Arguments:
- tokens: bfloat16 [8, 3, 32, 32, 1024], P('obj', None, 'plane', 'tile'), may hold values from -6 to 6
- gout: bfloat16 [8, 3, 128, 128, 128], P('obj', None, 'plane', 'tile'), may hold values from -6 to 6
- deconv_weight: bfloat16 [1024, 2048], replicated, may hold values from -0.1875 to 0.1875
- deconv_bias: float32 [128], replicated, may hold values from -4 to 4
- conv_kernels: bfloat16 [2, 1152, 128], replicated, may hold values from -0.1875 to 0.1875
- conv_biases: float32 [2, 128], replicated, may hold values from -4 to 4
Outputs:
- d_tokens: bfloat16 [8, 3, 32, 32, 1024], P('obj', None, 'plane', 'tile')
- d_deconv_weight: float32 [1024, 2048], P(('obj', 'plane', 'tile'))
- d_deconv_bias: float32 [128], replicated
- d_conv_kernels: float32 [2, 1152, 128], replicated
- d_conv_biases: float32 [2, 128], replicated
All inputs are finite; a program needn't handle non-finite values.
Results may differ from a plain program's by a relative error of at most 0.01.
Values may be sent and summed in bfloat16 or wider, within the bound.
No kernel may reach another device: no remote copies, remote signals or barrier semaphores. Data moves between devices by JAX's collectives and lax.ppermute only.
A program may use at most 192 MiB of HBM per device.

v0:
```python
import jax
import jax.numpy as jnp
from jax import lax
from jax.sharding import PartitionSpec as P


def padded_2(array, sides, width):
    for axis, dim in sides:
        size, length = (lax.axis_size(axis), array.shape[dim])
        up = [(i, (i + 1) % size) for i in range(size - 1)]
        down = [(j, i) for i, j in up]
        last = lax.slice_in_dim(array, length - width, length, axis=dim)
        initial = lax.slice_in_dim(array, 0, width, axis=dim)
        before = lax.ppermute(last, axis, up)
        after = lax.ppermute(initial, axis, down)
        array = jnp.concatenate([before, array, after], axis=dim)
    return array


def columns(padded, height, breadth, flipped):
    pieces = []
    for tap_y in range(3):
        for tap_x in range(3):
            shift_y = 2 - tap_y if flipped else tap_y
            shift_x = 2 - tap_x if flipped else tap_x
            pieces.append(padded[..., shift_y : shift_y + height, shift_x : shift_x + breadth, :])
    return jnp.concatenate(pieces, axis=-1)


def convolve(padded, kernel, height, breadth, flipped):
    gathered = columns(padded, height, breadth, flipped)
    products = jnp.dot(
        gathered.reshape(-1, gathered.shape[-1]), kernel, preferred_element_type=jnp.float32
    )
    return products.reshape(padded.shape[:-3] + (height, breadth, kernel.shape[1]))


def upsample(tokens_here, weight, offsets):
    planes, tok_rows, tok_cols, fan_width = tokens_here.shape
    products = jnp.dot(
        tokens_here.reshape(-1, fan_width), weight, preferred_element_type=jnp.float32
    )
    products = products.reshape(planes, tok_rows, tok_cols, 4, 4, -1).transpose(0, 1, 3, 2, 4, 5)
    return products.reshape(planes, 4 * tok_rows, 4 * tok_cols, -1) + offsets


def tap_layout(gradient):
    planes, height, breadth, channels = gradient.shape
    blocks = gradient.reshape(planes, height // 4, 4, breadth // 4, 4, channels).transpose(
        0, 1, 3, 2, 4, 5
    )
    return blocks.reshape(-1, 16 * channels)


def contexts(row_sum, col_sum, extent):
    row_mean = row_sum / extent
    col_mean = col_sum / extent
    row_ctx = jnp.stack([row_mean[1], row_mean[0], col_mean[0]])
    col_ctx = jnp.stack([row_mean[2], col_mean[2], col_mean[1]])
    return (row_ctx, col_ctx)


def adjoint_contexts(row_sum, col_sum, extent):
    row_adjoint = jnp.stack([row_sum[1], row_sum[0], col_sum[0]])
    col_adjoint = jnp.stack([row_sum[2], col_sum[2], col_sum[1]])
    return (row_adjoint / extent, col_adjoint / extent)


def flip_kernel(kernel):
    channels = kernel.shape[1]
    return kernel.reshape(9, channels, channels).transpose(0, 2, 1).reshape(9 * channels, channels)


def pooled_sums(row_part, col_part, row_start, col_start, extent):
    zero_index = jnp.zeros((), jnp.int32)
    row_full = lax.dynamic_update_slice(
        jnp.zeros((row_part.shape[0], extent, row_part.shape[2]), jnp.float32),
        row_part,
        (zero_index, row_start, zero_index),
    )
    col_full = lax.dynamic_update_slice(
        jnp.zeros((col_part.shape[0], extent, col_part.shape[2]), jnp.float32),
        col_part,
        (zero_index, col_start, zero_index),
    )
    result = lax.psum((row_full, col_full), ("plane", "tile"))
    return result


def object_pass(tokens_here, grad_out, deconv_weight, deconv_bias, conv_kernels, conv_biases):
    hidden = upsample(tokens_here, deconv_weight, deconv_bias)
    planes, height, breadth, channels = hidden.shape
    extent = height * lax.axis_size("plane")
    row_start = lax.axis_index("plane") * height
    col_start = lax.axis_index("tile") * breadth
    layers = conv_kernels.shape[0]
    stored = []
    for layer_index in range(layers):
        row_sum, col_sum = pooled_sums(
            jnp.sum(hidden, 2), jnp.sum(hidden, 1), row_start, col_start, extent
        )
        row_ctx, col_ctx = contexts(row_sum, col_sum, extent)
        row_band = lax.dynamic_slice_in_dim(row_ctx, row_start, height, 1)
        col_band = lax.dynamic_slice_in_dim(col_ctx, col_start, breadth, 1)
        preact = hidden + row_band[:, :, None, :] + col_band[:, None, :, :]
        activated = jax.nn.silu(preact).astype(jnp.bfloat16)
        padded = padded_2(activated, (("plane", 1), ("tile", 2)), 1)
        conv_out = convolve(padded, conv_kernels[layer_index], height, breadth, False)
        hidden = hidden + conv_out + conv_biases[layer_index]
        stored.append((preact, padded))
    gradient = grad_out.astype(jnp.float32)
    kernel_grads = []
    bias_grads = []
    for layer_index in reversed(range(layers)):
        preact, padded = stored[layer_index]
        grad_bf = gradient.astype(jnp.bfloat16)
        bias_grads.insert(0, jnp.sum(gradient, (0, 1, 2)))
        grad_pad = padded_2(grad_bf, (("plane", 1), ("tile", 2)), 1)
        act_grad = convolve(grad_pad, flip_kernel(conv_kernels[layer_index]), height, breadth, True)
        gathered = columns(padded, height, breadth, False)
        kernel_grads.insert(
            0,
            lax.dot_general(
                gathered.reshape(-1, gathered.shape[-1]),
                grad_bf.reshape(-1, channels),
                (((0,), (0,)), ((), ())),
                preferred_element_type=jnp.float32,
            ),
        )
        sigmoid_pre = jax.nn.sigmoid(preact)
        pre_grad = act_grad * sigmoid_pre * (1.0 + preact * (1.0 - sigmoid_pre))
        row_sum, col_sum = pooled_sums(
            jnp.sum(pre_grad, 2), jnp.sum(pre_grad, 1), row_start, col_start, extent
        )
        row_adjoint, col_adjoint = adjoint_contexts(row_sum, col_sum, extent)
        row_band = lax.dynamic_slice_in_dim(row_adjoint, row_start, height, 1)
        col_band = lax.dynamic_slice_in_dim(col_adjoint, col_start, breadth, 1)
        gradient = gradient + pre_grad + row_band[:, :, None, :] + col_band[:, None, :, :]
    grad_bf = gradient.astype(jnp.bfloat16)
    tap_grads = tap_layout(grad_bf)
    tok_grad = lax.dot_general(
        tap_grads, deconv_weight, (((1,), (1,)), ((), ())), preferred_element_type=jnp.float32
    )
    tok_grad = tok_grad.astype(jnp.bfloat16).reshape(tokens_here.shape)
    return (
        tok_grad,
        tap_grads,
        jnp.sum(gradient, (0, 1, 2)),
        jnp.stack(kernel_grads),
        jnp.stack(bias_grads),
    )


def per_device(tokens, gout, deconv_weight, deconv_bias, conv_kernels, conv_biases):
    tok_list = []
    tap_list = []
    flat_list = []
    bias_grad = jnp.zeros((deconv_bias.shape[0],), jnp.float32)
    kernel_sum = jnp.zeros(conv_kernels.shape, jnp.float32)
    conv_bias_sum = jnp.zeros(conv_biases.shape, jnp.float32)
    for object_index in range(tokens.shape[0]):
        tokens_here = tokens[object_index]
        tok_grad, tap_grads, bias_part, kernel_part, conv_bias_part = object_pass(
            tokens_here, gout[object_index], deconv_weight, deconv_bias, conv_kernels, conv_biases
        )
        tok_list.append(tok_grad)
        tap_list.append(tap_grads)
        flat_list.append(tokens_here.reshape(-1, tokens_here.shape[-1]))
        bias_grad = bias_grad + bias_part
        kernel_sum = kernel_sum + kernel_part
        conv_bias_sum = conv_bias_sum + conv_bias_part
    tok_out = jnp.stack(tok_list)
    tap_all = jnp.concatenate(tap_list, axis=0)
    tok_flat = jnp.concatenate(flat_list, axis=0)
    object_part = lax.psum_scatter(
        lax.dot_general(
            tok_flat, tap_all, (((0,), (0,)), ((), ())), preferred_element_type=jnp.float32
        ).astype(jnp.bfloat16),
        "obj",
        scatter_dimension=0,
        tiled=True,
    ).astype(jnp.float32)
    weight_grad = lax.psum_scatter(object_part, ("plane", "tile"), scatter_dimension=0, tiled=True)
    kernel_total, conv_bias_total, bias_total = lax.psum(
        (kernel_sum, conv_bias_sum, bias_grad), ("obj", "plane", "tile")
    )
    return (tok_out, weight_grad, bias_total, kernel_total, conv_bias_total)


def solution(mesh):
    placed = (
        P("obj", None, "plane", "tile", None),
        P("obj", None, "plane", "tile", None),
        P(),
        P(),
        P(),
        P(),
    )
    return jax.shard_map(
        per_device,
        mesh=mesh,
        in_specs=placed,
        out_specs=(
            P("obj", None, "plane", "tile", None),
            P(("obj", "plane", "tile"), None),
            P(),
            P(),
            P(),
        ),
        check_vma=False,
    )
```

profile of v0, /device:TPU:0, one launch (start us, length us, event | category | flops | bytes accessed | tf_op | source)
XLA Modules:
  0.0 781.6 jit_solution(1945525639712762014)
XLA Ops:
  7.2 5.1 fusion.89
  18.0 5.2 collective-permute-start.12
  24.5 7.7 dot_general.56
  32.2 7.5 copy.45
  43.8 4.3 add_reduce_fusion.2
  65.7 5.1 copy.35
  77.2 4.5 collective-permute-start.3
  127.0 5.1 collective-permute-start.4
  135.1 4.6 collective-permute-start.18
  141.0 4.5 collective-permute-start.6
  170.7 5.7 fusion.88
  176.4 10.6 %fusion.85 = (f32[3,64,128]{2,1,0:T(8,128)S(1)}, f32[3,32,128]{2,1,0:T(8,128)S(1)}, f32[3,32,64,128]{3,2,1,0:T(8,128)}) fusion(f32[128]{0:T(128)S(1)} %slice_bitcast_fusion, bf16[3,32,64,1152]{3,2,1,0:T(8,128)(2,1)} %slice_dynamic-update-slice_fusion.36, bf16[2,1152,128]{2,1,0:T(8,128)(2,1)S(1)} %copy-done.25, f32[3,32,64,128]{3,2,1,0:T(8,128)S(1)} %bitcast.149, ...), kind=kOutput, calls=%fused_computation.314 | convolution fusion | flops 1815834624 | bytes 20890624 | tf_op jit(solution)/shard_map/dot_general | solution.py:32
  193.7 53.1 %all-reduce.17.cloned.1.call-done = (f32[3,128,128]{2,1,0:T(8,128)}, f32[3,128,128]{2,1,0:T(8,128)}, f32[3,128,128]{2,1,0:T(8,128)}, f32[3,128,128]{2,1,0:T(8,128)}) async-done(((f32[3,128,128]{2,1,0:T(8,128)}, f32[3,128,128]{2,1,0:T(8,128)}, f32[3,128,128]{2,1,0:T(8,128)}, f32[3,128,128]{2,1,0:T(8,128)}), (f32[3,128,128]{2,1,0:T(8,128)}, f32[3,128,128]{2,1,0:T(8,128)}, f32[3,128,128]{2,1,0:T(8,128)}, ...) | async-done | bytes 786448 | tf_op jit(solution)/shard_map/psum | solution.py:86
  253.7 12.2 %fusion.87 = (f32[3,64,128]{2,1,0:T(8,128)S(1)}, f32[3,32,128]{2,1,0:T(8,128)S(1)}, f32[3,32,64,128]{3,2,1,0:T(8,128)}) fusion(f32[3,64,128]{2,1,0:T(8,128)S(1)} %fusion.41, f32[3,32,64,128]{3,2,1,0:T(8,128)S(1)} %copy-done.13, f32[3,32,128]{2,1,0:T(8,128)S(1)} %fusion.61, bf16[3,32,64,1152]{3,2,1,0:T(8,128)(2,1)} %slice_dynamic-update-slice_fusion.24, ...), kind=kOutput, calls=%fused_computation.316 | convolution fusion | flops 1821339648 | bytes 21037056 | tf_op jit(solution)/shard_map/dot_general | solution.py:32
  266.8 6.6 fusion.84
  289.6 4.5 collective-permute-start.26
  297.1 5.7 collective-permute-start.30
  313.3 32.7 %all-reduce.15.cloned.1.call-done = (f32[3,128,128]{2,1,0:T(8,128)}, f32[3,128,128]{2,1,0:T(8,128)}, f32[3,128,128]{2,1,0:T(8,128)}, f32[3,128,128]{2,1,0:T(8,128)}) async-done(((f32[3,128,128]{2,1,0:T(8,128)}, f32[3,128,128]{2,1,0:T(8,128)}, f32[3,128,128]{2,1,0:T(8,128)}, f32[3,128,128]{2,1,0:T(8,128)}), (f32[3,128,128]{2,1,0:T(8,128)}, f32[3,128,128]{2,1,0:T(8,128)}, f32[3,128,128]{2,1,0:T(8,128)}, ...) | async-done | bytes 786448 | tf_op jit(solution)/shard_map/psum | solution.py:86
  349.8 5.2 fusion.82
  366.9 4.5 collective-permute-start.11
  397.2 6.5 fusion.86
  403.7 11.7 %fusion.83 = (f32[3,64,128]{2,1,0:T(8,128)S(1)}, f32[3,32,128]{2,1,0:T(8,128)S(1)}, f32[3,32,64,128]{3,2,1,0:T(8,128)}) fusion(f32[3,64,128]{2,1,0:T(8,128)S(1)} %copy-done.46, f32[3,32,128]{2,1,0:T(8,128)S(1)} %copy-done.52, f32[3,32,64,128]{3,2,1,0:T(8,128)S(1)} %bitcast.150, f32[128]{0:T(128)S(1)} %copy-done.55, ...), kind=kOutput, calls=%fused_computation.312 | convolution fusion | flops 1822126080 | bytes 21037568 | tf_op jit(solution)/shard_map/dot_general | solution.py:32
  425.1 56.2 %all-reduce.13.cloned.1.call-done = (f32[3,128,128]{2,1,0:T(8,128)}, f32[3,128,128]{2,1,0:T(8,128)}, f32[3,128,128]{2,1,0:T(8,128)}, f32[3,128,128]{2,1,0:T(8,128)}) async-done(((f32[3,128,128]{2,1,0:T(8,128)}, f32[3,128,128]{2,1,0:T(8,128)}, f32[3,128,128]{2,1,0:T(8,128)}, f32[3,128,128]{2,1,0:T(8,128)}), (f32[3,128,128]{2,1,0:T(8,128)}, f32[3,128,128]{2,1,0:T(8,128)}, f32[3,128,128]{2,1,0:T(8,128)}, ...) | async-done | bytes 786448 | tf_op jit(solution)/shard_map/psum | solution.py:86
  485.1 7.8 fusion.79
  505.7 7.8 convolution_convert_fusion
  536.0 5.1 copy-done.54
  541.0 7.3 convolution_bitcast_fusion.3
  548.4 7.5 convolution_bitcast_fusion.2
  565.1 24.8 %reduce-scatter.3.cloned.1.call-done = bf16[256,2048]{1,0:T(8,128)(2,1)} async-done(((bf16[1024,2048]{1,0:T(8,128)(2,1)}), bf16[256,2048]{1,0:T(8,128)(2,1)}) %reduce-scatter.3.cloned.1.call-update) | async-done | bytes 1048592 | tf_op jit(solution)/shard_map/reduce_scatter | solution.py:175
  592.7 41.2 %all-reduce = (f32[128]{0:T(128)}, f32[2,128]{1,0:T(2,128)}) all-reduce(f32[128]{0:T(128)S(1)} %add.360, f32[2,128]{1,0:T(2,128)S(1)} %maximum_add_fusion.1), channel_id=1, replica_groups=mesh['obj'=4,'plane'=4,'tile'=2] {'obj','plane','tile'}, use_global_device_ids=true, to_apply=%region_36.37 | all-reduce | flops 384 | bytes 3072 | tf_op jit(solution)/shard_map/psum | solution.py:184
  641.2 87.1 %all-reduce.11.cloned.1.call-done = f32[2,1152,128]{2,1,0:T(8,128)} async-done(((f32[2,1152,128]{2,1,0:T(8,128)}), f32[2,1152,128]{2,1,0:T(8,128)}) %all-reduce.11.cloned.1.call-update) | async-done | bytes 1179664 | tf_op jit(solution)/shard_map/psum | solution.py:184
  728.2 43.9 %reduce-scatter.5.cloned.1.call-done = f32[32,2048]{1,0:T(8,128)} async-done(((f32[256,2048]{1,0:T(8,128)}), f32[32,2048]{1,0:T(8,128)}) %reduce-scatter.5.cloned.1.call-update) | async-done | bytes 262160 | tf_op jit(solution)/shard_map/reduce_scatter | solution.py:183
  (402 shorter events, 263.8 us)
Async XLA Ops:
  7.2 107.7 %all-reduce.19.cloned.1.call-start = ((), (), s32[]{:S(2)}) async-start(), calls=%async_computation.8 | async-start | bytes 1572864 | tf_op jit(solution)/shard_map/psum | solution.py:86
  13.1 63.3 %collective-permute-start = (bf16[3,1,64,128]{3,2,1,0:T(8,128)(2,1)}, bf16[3,1,64,128]{3,2,1,0:T(8,128)(2,1)}, u32[]{:S(2)}, u32[]{:S(2)}) collective-permute-start(bf16[3,1,64,128]{3,2,1,0:T(8,128)(2,1)} %get-tuple-element.101), channel_id=1, source_target_pairs={{0,2},{2,4},{4,6},{1,3},{3,5},{5,7},{8,10},{10,12},{12,14},{9,11},... | collective-permute-start | bytes 147464 | tf_op jit(solution)/shard_map/ppermute | solution.py:14
  16.1 60.3 %collective-permute-start.1 = (bf16[3,1,64,128]{3,2,1,0:T(8,128)(2,1)}, bf16[3,1,64,128]{3,2,1,0:T(8,128)(2,1)}, u32[]{:S(2)}, u32[]{:S(2)}) collective-permute-start(bf16[3,1,64,128]{3,2,1,0:T(8,128)(2,1)} %get-tuple-element.102), channel_id=1, source_target_pairs={{2,0},{4,2},{6,4},{3,1},{5,3},{7,5},{10,8},{12,10},{14,12},{11,9},... | collective-permute-start | bytes 147464 | tf_op jit(solution)/shard_map/ppermute | solution.py:15
  18.0 52.8 %collective-permute-start.12 = (bf16[3,1,64,128]{3,2,1,0:T(8,128)(2,1)}, bf16[3,1,64,128]{3,2,1,0:T(8,128)(2,1)}, u32[]{:S(2)}, u32[]{:S(2)}) collective-permute-start(bf16[3,1,64,128]{3,2,1,0:T(8,128)(2,1)} %get-tuple-element.105), channel_id=1, source_target_pairs={{0,2},{2,4},{4,6},{1,3},{3,5},{5,7},{8,10},{10,12},{12,14},{9,11},... | collective-permute-start | bytes 147464 | tf_op jit(solution)/shard_map/ppermute | solution.py:14
  23.2 47.7 %collective-permute-start.13 = (bf16[3,1,64,128]{3,2,1,0:T(8,128)(2,1)}, bf16[3,1,64,128]{3,2,1,0:T(8,128)(2,1)}, u32[]{:S(2)}, u32[]{:S(2)}) collective-permute-start(bf16[3,1,64,128]{3,2,1,0:T(8,128)(2,1)} %get-tuple-element.106), channel_id=1, source_target_pairs={{2,0},{4,2},{6,4},{3,1},{5,3},{7,5},{10,8},{12,10},{14,12},{11,9},... | collective-permute-start | bytes 147464 | tf_op jit(solution)/shard_map/ppermute | solution.py:15
  55.0 191.8 %all-reduce.17.cloned.1.call-start = ((), (), s32[]{:S(2)}) async-start(), calls=%async_computation.7 | async-start | bytes 1572864 | tf_op jit(solution)/shard_map/psum | solution.py:86
  71.7 11.8 %collective-permute-start.15 = (bf16[3,34,1,128]{3,2,1,0:T(2,128)(2,1)S(1)}, bf16[3,34,1,128]{3,2,1,0:T(2,128)(2,1)S(1)}, u32[]{:S(2)}, u32[]{:S(2)}) collective-permute-start(bf16[3,34,1,128]{3,2,1,0:T(2,128)(2,1)S(1)} %get-tuple-element.85), channel_id=1, source_target_pairs={{0,1},{2,3},{4,5},{6,7},{8,9},{10,11},{12,13},{14,15},{16,17},{18,... | collective-permute-start | bytes 78344 | tf_op jit(solution)/shard_map/ppermute | solution.py:14
  75.0 8.5 %collective-permute-start.14 = (bf16[3,34,1,128]{3,2,1,0:T(2,128)(2,1)S(1)}, bf16[3,34,1,128]{3,2,1,0:T(2,128)(2,1)S(1)}, u32[]{:S(2)}, u32[]{:S(2)}) collective-permute-start(bf16[3,34,1,128]{3,2,1,0:T(2,128)(2,1)S(1)} %get-tuple-element.86), channel_id=1, source_target_pairs={{1,0},{3,2},{5,4},{7,6},{9,8},{11,10},{13,12},{15,14},{17,16},{19,... | collective-permute-start | bytes 78344 | tf_op jit(solution)/shard_map/ppermute | solution.py:15
  77.2 17.2 %collective-permute-start.3 = (bf16[3,34,1,128]{3,2,1,0:T(2,128)(2,1)S(1)}, bf16[3,34,1,128]{3,2,1,0:T(2,128)(2,1)S(1)}, u32[]{:S(2)}, u32[]{:S(2)}) collective-permute-start(bf16[3,34,1,128]{3,2,1,0:T(2,128)(2,1)S(1)} %get-tuple-element.77), channel_id=1, source_target_pairs={{0,1},{2,3},{4,5},{6,7},{8,9},{10,11},{12,13},{14,15},{16,17},{18,... | collective-permute-start | bytes 78344 | tf_op jit(solution)/shard_map/ppermute | solution.py:14
  81.7 12.6 %collective-permute-start.2 = (bf16[3,34,1,128]{3,2,1,0:T(2,128)(2,1)S(1)}, bf16[3,34,1,128]{3,2,1,0:T(2,128)(2,1)S(1)}, u32[]{:S(2)}, u32[]{:S(2)}) collective-permute-start(bf16[3,34,1,128]{3,2,1,0:T(2,128)(2,1)S(1)} %get-tuple-element.78), channel_id=1, source_target_pairs={{1,0},{3,2},{5,4},{7,6},{9,8},{11,10},{13,12},{15,14},{17,16},{19,... | collective-permute-start | bytes 78344 | tf_op jit(solution)/shard_map/ppermute | solution.py:15
  122.8 10.8 %collective-permute-start.16 = (bf16[3,1,64,128]{3,2,1,0:T(8,128)(2,1)S(1)}, bf16[3,1,64,128]{3,2,1,0:T(8,128)(2,1)S(1)}, u32[]{:S(2)}, u32[]{:S(2)}) collective-permute-start(bf16[3,1,64,128]{3,2,1,0:T(8,128)(2,1)S(1)} %get-tuple-element.107), channel_id=1, source_target_pairs={{0,2},{2,4},{4,6},{1,3},{3,5},{5,7},{8,10},{10,12},{12,14},{9,11},... | collective-permute-start | bytes 147464 | tf_op jit(solution)/shard_map/ppermute | solution.py:14
  127.0 12.6 %collective-permute-start.4 = (bf16[3,1,64,128]{3,2,1,0:T(8,128)(2,1)S(1)}, bf16[3,1,64,128]{3,2,1,0:T(8,128)(2,1)S(1)}, u32[]{:S(2)}, u32[]{:S(2)}) collective-permute-start(bf16[3,1,64,128]{3,2,1,0:T(8,128)(2,1)S(1)} %get-tuple-element.103), channel_id=1, source_target_pairs={{0,2},{2,4},{4,6},{1,3},{3,5},{5,7},{8,10},{10,12},{12,14},{9,11},... | collective-permute-start | bytes 147464 | tf_op jit(solution)/shard_map/ppermute | solution.py:14
  133.8 11.8 %collective-permute-start.19 = (bf16[3,34,1,128]{3,2,1,0:T(2,128)(2,1)S(1)}, bf16[3,34,1,128]{3,2,1,0:T(2,128)(2,1)S(1)}, u32[]{:S(2)}, u32[]{:S(2)}) collective-permute-start(bf16[3,34,1,128]{3,2,1,0:T(2,128)(2,1)S(1)} %get-tuple-element.89), channel_id=1, source_target_pairs={{1,0},{3,2},{5,4},{7,6},{9,8},{11,10},{13,12},{15,14},{17,16},{19,... | collective-permute-start | bytes 78344 | tf_op jit(solution)/shard_map/ppermute | solution.py:15
  135.1 10.5 %collective-permute-start.18 = (bf16[3,34,1,128]{3,2,1,0:T(2,128)(2,1)S(1)}, bf16[3,34,1,128]{3,2,1,0:T(2,128)(2,1)S(1)}, u32[]{:S(2)}, u32[]{:S(2)}) collective-permute-start(bf16[3,34,1,128]{3,2,1,0:T(2,128)(2,1)S(1)} %get-tuple-element.90), channel_id=1, source_target_pairs={{0,1},{2,3},{4,5},{6,7},{8,9},{10,11},{12,13},{14,15},{16,17},{18,... | collective-permute-start | bytes 78344 | tf_op jit(solution)/shard_map/ppermute | solution.py:14
  139.7 13.5 %collective-permute-start.7 = (bf16[3,34,1,128]{3,2,1,0:T(2,128)(2,1)S(1)}, bf16[3,34,1,128]{3,2,1,0:T(2,128)(2,1)S(1)}, u32[]{:S(2)}, u32[]{:S(2)}) collective-permute-start(bf16[3,34,1,128]{3,2,1,0:T(2,128)(2,1)S(1)} %get-tuple-element.81), channel_id=1, source_target_pairs={{1,0},{3,2},{5,4},{7,6},{9,8},{11,10},{13,12},{15,14},{17,16},{19,... | collective-permute-start | bytes 78344 | tf_op jit(solution)/shard_map/ppermute | solution.py:15
  141.0 12.2 %collective-permute-start.6 = (bf16[3,34,1,128]{3,2,1,0:T(2,128)(2,1)S(1)}, bf16[3,34,1,128]{3,2,1,0:T(2,128)(2,1)S(1)}, u32[]{:S(2)}, u32[]{:S(2)}) collective-permute-start(bf16[3,34,1,128]{3,2,1,0:T(2,128)(2,1)S(1)} %get-tuple-element.82), channel_id=1, source_target_pairs={{0,1},{2,3},{4,5},{6,7},{8,9},{10,11},{12,13},{14,15},{16,17},{18,... | collective-permute-start | bytes 78344 | tf_op jit(solution)/shard_map/ppermute | solution.py:14
  188.0 158.0 %all-reduce.15.cloned.1.call-start = ((), (), s32[]{:S(2)}) async-start(), calls=%async_computation.6 | async-start | bytes 1572864 | tf_op jit(solution)/shard_map/psum | solution.py:86
  274.0 13.4 %collective-permute-start.24 = (bf16[3,1,64,128]{3,2,1,0:T(8,128)(2,1)}, bf16[3,1,64,128]{3,2,1,0:T(8,128)(2,1)}, u32[]{:S(2)}, u32[]{:S(2)}) collective-permute-start(bf16[3,1,64,128]{3,2,1,0:T(8,128)(2,1)} %get-tuple-element.93), channel_id=1, source_target_pairs={{0,2},{2,4},{4,6},{1,3},{3,5},{5,7},{8,10},{10,12},{12,14},{9,11},... | collective-permute-start | bytes 147464 | tf_op jit(solution)/shard_map/ppermute | solution.py:14
  275.9 11.5 %collective-permute-start.25 = (bf16[3,1,64,128]{3,2,1,0:T(8,128)(2,1)}, bf16[3,1,64,128]{3,2,1,0:T(8,128)(2,1)}, u32[]{:S(2)}, u32[]{:S(2)}) collective-permute-start(bf16[3,1,64,128]{3,2,1,0:T(8,128)(2,1)} %get-tuple-element.94), channel_id=1, source_target_pairs={{2,0},{4,2},{6,4},{3,1},{5,3},{7,5},{10,8},{12,10},{14,12},{11,9},... | collective-permute-start | bytes 147464 | tf_op jit(solution)/shard_map/ppermute | solution.py:15
  277.9 16.3 %collective-permute-start.28 = (bf16[3,1,64,128]{3,2,1,0:T(8,128)(2,1)}, bf16[3,1,64,128]{3,2,1,0:T(8,128)(2,1)}, u32[]{:S(2)}, u32[]{:S(2)}) collective-permute-start(bf16[3,1,64,128]{3,2,1,0:T(8,128)(2,1)} %get-tuple-element.91), channel_id=1, source_target_pairs={{0,2},{2,4},{4,6},{1,3},{3,5},{5,7},{8,10},{10,12},{12,14},{9,11},... | collective-permute-start | bytes 147464 | tf_op jit(solution)/shard_map/ppermute | solution.py:14
  282.0 12.2 %collective-permute-start.29 = (bf16[3,1,64,128]{3,2,1,0:T(8,128)(2,1)}, bf16[3,1,64,128]{3,2,1,0:T(8,128)(2,1)}, u32[]{:S(2)}, u32[]{:S(2)}) collective-permute-start(bf16[3,1,64,128]{3,2,1,0:T(8,128)(2,1)} %get-tuple-element.92), channel_id=1, source_target_pairs={{2,0},{4,2},{6,4},{3,1},{5,3},{7,5},{10,8},{12,10},{14,12},{11,9},... | collective-permute-start | bytes 147464 | tf_op jit(solution)/shard_map/ppermute | solution.py:15
  287.4 194.0 %all-reduce.13.cloned.1.call-start = ((), (), s32[]{:S(2)}) async-start(), calls=%async_computation.5 | async-start | bytes 1572864 | tf_op jit(solution)/shard_map/psum | solution.py:86
  288.3 14.6 %collective-permute-start.27 = (bf16[3,34,1,128]{3,2,1,0:T(2,128)(2,1)S(1)}, bf16[3,34,1,128]{3,2,1,0:T(2,128)(2,1)S(1)}, u32[]{:S(2)}, u32[]{:S(2)}) collective-permute-start(bf16[3,34,1,128]{3,2,1,0:T(2,128)(2,1)S(1)} %get-tuple-element.65), channel_id=1, source_target_pairs={{1,0},{3,2},{5,4},{7,6},{9,8},{11,10},{13,12},{15,14},{17,16},{19,... | collective-permute-start | bytes 78344 | tf_op jit(solution)/shard_map/ppermute | solution.py:15
  289.6 13.3 %collective-permute-start.26 = (bf16[3,34,1,128]{3,2,1,0:T(2,128)(2,1)S(1)}, bf16[3,34,1,128]{3,2,1,0:T(2,128)(2,1)S(1)}, u32[]{:S(2)}, u32[]{:S(2)}) collective-permute-start(bf16[3,34,1,128]{3,2,1,0:T(2,128)(2,1)S(1)} %get-tuple-element.66), channel_id=1, source_target_pairs={{0,1},{2,3},{4,5},{6,7},{8,9},{10,11},{12,13},{14,15},{16,17},{18,... | collective-permute-start | bytes 78344 | tf_op jit(solution)/shard_map/ppermute | solution.py:14
  295.6 226.6 %collective-permute-start.31 = (bf16[3,34,1,128]{3,2,1,0:T(2,128)(2,1)}, bf16[3,34,1,128]{3,2,1,0:T(2,128)(2,1)}, u32[]{:S(2)}, u32[]{:S(2)}) collective-permute-start(bf16[3,34,1,128]{3,2,1,0:T(2,128)(2,1)} %get-tuple-element.61), channel_id=1, source_target_pairs={{1,0},{3,2},{5,4},{7,6},{9,8},{11,10},{13,12},{15,14},{17,16},{19,... | collective-permute-start | bytes 78344 | tf_op jit(solution)/shard_map/ppermute | solution.py:15
  297.1 225.1 %collective-permute-start.30 = (bf16[3,34,1,128]{3,2,1,0:T(2,128)(2,1)}, bf16[3,34,1,128]{3,2,1,0:T(2,128)(2,1)}, u32[]{:S(2)}, u32[]{:S(2)}) collective-permute-start(bf16[3,34,1,128]{3,2,1,0:T(2,128)(2,1)} %get-tuple-element.62), channel_id=1, source_target_pairs={{0,1},{2,3},{4,5},{6,7},{8,9},{10,11},{12,13},{14,15},{16,17},{18,... | collective-permute-start | bytes 78344 | tf_op jit(solution)/shard_map/ppermute | solution.py:14
  363.1 8.3 %collective-permute-start.23 = (bf16[3,34,1,128]{3,2,1,0:T(2,128)(2,1)S(1)}, bf16[3,34,1,128]{3,2,1,0:T(2,128)(2,1)S(1)}, u32[]{:S(2)}, u32[]{:S(2)}) collective-permute-start(bf16[3,34,1,128]{3,2,1,0:T(2,128)(2,1)S(1)} %get-tuple-element.73), channel_id=1, source_target_pairs={{0,1},{2,3},{4,5},{6,7},{8,9},{10,11},{12,13},{14,15},{16,17},{18,... | collective-permute-start | bytes 78344 | tf_op jit(solution)/shard_map/ppermute | solution.py:14
  366.9 13.4 %collective-permute-start.11 = (bf16[3,34,1,128]{3,2,1,0:T(2,128)(2,1)S(1)}, bf16[3,34,1,128]{3,2,1,0:T(2,128)(2,1)S(1)}, u32[]{:S(2)}, u32[]{:S(2)}) collective-permute-start(bf16[3,34,1,128]{3,2,1,0:T(2,128)(2,1)S(1)} %get-tuple-element.69), channel_id=1, source_target_pairs={{0,1},{2,3},{4,5},{6,7},{8,9},{10,11},{12,13},{14,15},{16,17},{18,... | collective-permute-start | bytes 78344 | tf_op jit(solution)/shard_map/ppermute | solution.py:14
  371.5 8.8 %collective-permute-start.10 = (bf16[3,34,1,128]{3,2,1,0:T(2,128)(2,1)S(1)}, bf16[3,34,1,128]{3,2,1,0:T(2,128)(2,1)S(1)}, u32[]{:S(2)}, u32[]{:S(2)}) collective-permute-start(bf16[3,34,1,128]{3,2,1,0:T(2,128)(2,1)S(1)} %get-tuple-element.70), channel_id=1, source_target_pairs={{1,0},{3,2},{5,4},{7,6},{9,8},{11,10},{13,12},{15,14},{17,16},{19,... | collective-permute-start | bytes 78344 | tf_op jit(solution)/shard_map/ppermute | solution.py:15
  420.7 169.1 %reduce-scatter.3.cloned.1.call-start = ((), (), s32[]{:S(2)}) async-start(), calls=%async_computation.2 | async-start | bytes 5242880 | tf_op jit(solution)/shard_map/reduce_scatter | solution.py:175
  513.5 214.7 %all-reduce.11.cloned.1.call-start = ((), (), s32[]{:S(2)}) async-start(), calls=%async_computation.4 | async-start | bytes 2359296 | tf_op jit(solution)/shard_map/psum | solution.py:184
  565.0 207.1 %reduce-scatter.5.cloned.1.call-start = ((), (), s32[]{:S(2)}) async-start(), calls=%async_computation.3 | async-start | bytes 2359296 | tf_op jit(solution)/shard_map/reduce_scatter | solution.py:183
  (76 other events, 755.3 us)
Sparse Core Ops, SparseCore 0:
  55.1 59.0 all-reduce.18
  188.1 58.6 all-reduce.16
  287.5 58.4 all-reduce.14
  420.9 60.4 all-reduce.12
  513.6 76.1 reduce-scatter.2
  595.6 132.5 all-reduce.10
  732.1 40.0 reduce-scatter.4
where the time goes:
time: 792 us; the launch traced here: 782 us
  waiting for transfers between devices  298 us (38%)
  local copies, waits for them, and re-layouts  158 us (20%)
  matrix products  98 us (12%)
  other arithmetic  85.8 us (11%)
  starting transfers between devices  84.3 us (11%)
  blocking collectives  41.2 us (5%)
  between operations  16.3 us (2%)
    psum x4, waiting for transfers between devices, pooled_sums(): result = lax.psum((row_full, col_full), ('plane', 'tile'))  142 us
    psum x1, waiting for transfers between devices, per_device(): lax.psum((kernel_sum, conv_bias_sum, bias_grad), ('obj', 'plane', 'tile'))  87.1 us
    unnamed x184, local copies, waits for them, and re-layouts  71.6 us
    ppermute x16, starting transfers between devices, padded_2(): before = lax.ppermute(last, axis, up)  61.8 us
    dot_general x6, matrix products, convolve(): jnp.dot(gathered.reshape(-1, gathered.shape[-1]), kernel, preferred_eleme...  53.3 us
    reduce_scatter x1, waiting for transfers between devices, per_device(): lax.psum_scatter(object_part, ('plane', 'tile'), scatter_dimension=0, til...  43.9 us
    psum x1, blocking collectives, per_device(): lax.psum((kernel_sum, conv_bias_sum, bias_grad), ('obj', 'plane', 'tile'))  41.2 us
    concatenate x16, other arithmetic, padded_2(): array = jnp.concatenate([before, array, after], axis=dim)  26.6 us
  transfers between devices with their start and end apart: 39, of which 6 were waited for; matrix products, arithmetic and copies ran while one was open for 32% of the time, Pallas kernels for 0%

commit v1 on v0

--- a/solution.py
+++ b/solution.py
@@ -83,7 +83,7 @@
         col_part,
         (zero_index, col_start, zero_index),
     )
-    result = lax.psum((row_full, col_full), ("plane", "tile"))
+    result = lax.psum(lax.psum((row_full, col_full), "tile"), "plane")
     return result
 
 

time: 792 us -> 867 us (1.095)
  waiting for transfers between devices: 298 us -> 367 us
    psum x4 -> x8, waiting for transfers between devices: 142 us -> 209 us  [pooled_sums(): result = lax.psum(lax.psum((row_full, col_full), 'tile'), 'plane')]
    unnamed x184 -> x194, local copies, waits for them, and re-layouts: 71.6 us -> 76.5 us
  transfers between devices with their start and end apart: 39 -> 43, of which waited for: 6 -> 10; matrix products, arithmetic and copies ran while one was open for 32% -> 32% of each run, Pallas kernels for 0% -> 0%
where the time goes in v1:
time: 867 us; the launch traced here: 857 us
  waiting for transfers between devices  367 us (42%)
  local copies, waits for them, and re-layouts  165 us (19%)
  matrix products  97.8 us (11%)
  other arithmetic  88.2 us (10%)
  starting transfers between devices  81.9 us (9%)
  blocking collectives  41.1 us (5%)
  between operations  16 us (2%)
    psum x8, waiting for transfers between devices, pooled_sums(): result = lax.psum(lax.psum((row_full, col_full), 'tile'), 'plane')  209 us
    psum x1, waiting for transfers between devices, per_device(): lax.psum((kernel_sum, conv_bias_sum, bias_grad), ('obj', 'plane', 'tile'))  87.3 us
    unnamed x194, local copies, waits for them, and re-layouts  76.5 us
    ppermute x16, starting transfers between devices, padded_2(): before = lax.ppermute(last, axis, up)  59.4 us
    dot_general x6, matrix products, convolve(): jnp.dot(gathered.reshape(-1, gathered.shape[-1]), kernel, preferred_eleme...  52.9 us
    reduce_scatter x1, waiting for transfers between devices, per_device(): lax.psum_scatter(object_part, ('plane', 'tile'), scatter_dimension=0, til...  43.9 us
    psum x1, blocking collectives, per_device(): lax.psum((kernel_sum, conv_bias_sum, bias_grad), ('obj', 'plane', 'tile'))  41.1 us
    concatenate x16, other arithmetic, padded_2(): array = jnp.concatenate([before, array, after], axis=dim)  27.8 us
  transfers between devices with their start and end apart: 43, of which 10 were waited for; matrix products, arithmetic and copies ran while one was open for 32% of the time, Pallas kernels for 0%

profile of v1, /device:TPU:0, one launch (start us, length us, event | category | flops | bytes accessed | tf_op | source)
XLA Modules:
  0.0 857.0 jit_solution(18420707119972364316)
XLA Ops:
  7.2 5.2 fusion.89
  18.0 5.2 collective-permute-start.12
  24.4 7.7 dot_general.56
  32.1 7.5 copy.45
  65.8 5.1 copy.35
  103.2 5.0 copy-done.58
  115.4 33.8 %all-reduce.27.cloned.1.call-done = (f32[3,128,128]{2,1,0:T(8,128)}, f32[3,128,128]{2,1,0:T(8,128)}, f32[3,128,128]{2,1,0:T(8,128)}, f32[3,128,128]{2,1,0:T(8,128)}) async-done(((f32[3,128,128]{2,1,0:T(8,128)}, f32[3,128,128]{2,1,0:T(8,128)}, f32[3,128,128]{2,1,0:T(8,128)}, f32[3,128,128]{2,1,0:T(8,128)}), (f32[3,128,128]{2,1,0:T(8,128)}, f32[3,128,128]{2,1,0:T(8,128)}, f32[3,128,128]{2,1,0:T(8,128)}, ...) | async-done | bytes 786448 | tf_op jit(solution)/shard_map/psum | solution.py:86
  171.9 4.7 collective-permute-start.6
  202.1 5.7 fusion.88
  207.8 10.8 %fusion.85 = (f32[3,64,128]{2,1,0:T(8,128)S(1)}, f32[3,32,128]{2,1,0:T(8,128)S(1)}, f32[3,32,64,128]{3,2,1,0:T(8,128)}) fusion(f32[128]{0:T(128)S(1)} %slice_bitcast_fusion, bf16[3,32,64,1152]{3,2,1,0:T(8,128)(2,1)} %slice_dynamic-update-slice_fusion.36, bf16[2,1152,128]{2,1,0:T(8,128)(2,1)S(1)} %copy-done.27, f32[3,32,64,128]{3,2,1,0:T(8,128)S(1)} %bitcast.149, ...), kind=kOutput, calls=%fused_computation.314 | convolution fusion | flops 1815834624 | bytes 20890624 | tf_op jit(solution)/shard_map/dot_general | solution.py:32
  230.3 30.7 %all-reduce.33.cloned.1.call-done = (f32[3,128,128]{2,1,0:T(8,128)}, f32[3,128,128]{2,1,0:T(8,128)}, f32[3,128,128]{2,1,0:T(8,128)}, f32[3,128,128]{2,1,0:T(8,128)}) async-done(((f32[3,128,128]{2,1,0:T(8,128)}, f32[3,128,128]{2,1,0:T(8,128)}, f32[3,128,128]{2,1,0:T(8,128)}, f32[3,128,128]{2,1,0:T(8,128)}), (f32[3,128,128]{2,1,0:T(8,128)}, f32[3,128,128]{2,1,0:T(8,128)}, f32[3,128,128]{2,1,0:T(8,128)}, ...) | async-done | bytes 786448 | tf_op jit(solution)/shard_map/psum | solution.py:86
  265.1 33.3 %all-reduce.25.cloned.1.call-done = (f32[3,128,128]{2,1,0:T(8,128)}, f32[3,128,128]{2,1,0:T(8,128)}, f32[3,128,128]{2,1,0:T(8,128)}, f32[3,128,128]{2,1,0:T(8,128)}) async-done(((f32[3,128,128]{2,1,0:T(8,128)}, f32[3,128,128]{2,1,0:T(8,128)}, f32[3,128,128]{2,1,0:T(8,128)}, f32[3,128,128]{2,1,0:T(8,128)}), (f32[3,128,128]{2,1,0:T(8,128)}, f32[3,128,128]{2,1,0:T(8,128)}, f32[3,128,128]{2,1,0:T(8,128)}, ...) | async-done | bytes 786448 | tf_op jit(solution)/shard_map/psum | solution.py:86
  309.4 11.7 %fusion.84 = (f32[3,64,128]{2,1,0:T(8,128)S(1)}, f32[3,32,128]{2,1,0:T(8,128)S(1)}, f32[3,32,64,128]{3,2,1,0:T(8,128)}) fusion(f32[3,64,128]{2,1,0:T(8,128)S(1)} %fusion.51, f32[3,32,64,128]{3,2,1,0:T(8,128)S(1)} %copy-done.12, f32[3,32,128]{2,1,0:T(8,128)S(1)} %fusion.71, bf16[3,32,64,1152]{3,2,1,0:T(8,128)(2,1)} %slice_dynamic-update-slice_fusion.42, ...), kind=kOutput, calls=%fused_computation.313 | convolution fusion | flops 1821339648 | bytes 21037056 | tf_op jit(solution)/shard_map/dot_general | solution.py:32
  321.1 6.5 fusion.87
  339.3 5.2 collective-permute-start.26
  344.4 22.2 %all-reduce.31.cloned.1.call-done = (f32[3,128,128]{2,1,0:T(8,128)}, f32[3,128,128]{2,1,0:T(8,128)}, f32[3,128,128]{2,1,0:T(8,128)}, f32[3,128,128]{2,1,0:T(8,128)}) async-done(((f32[3,128,128]{2,1,0:T(8,128)}, f32[3,128,128]{2,1,0:T(8,128)}, f32[3,128,128]{2,1,0:T(8,128)}, f32[3,128,128]{2,1,0:T(8,128)}), (f32[3,128,128]{2,1,0:T(8,128)}, f32[3,128,128]{2,1,0:T(8,128)}, f32[3,128,128]{2,1,0:T(8,128)}, ...) | async-done | bytes 786448 | tf_op jit(solution)/shard_map/psum | solution.py:86
  369.0 5.8 collective-permute-start.30
  379.2 24.9 %all-reduce.23.cloned.1.call-done = (f32[3,128,128]{2,1,0:T(8,128)}, f32[3,128,128]{2,1,0:T(8,128)}, f32[3,128,128]{2,1,0:T(8,128)}, f32[3,128,128]{2,1,0:T(8,128)}) async-done(((f32[3,128,128]{2,1,0:T(8,128)}, f32[3,128,128]{2,1,0:T(8,128)}, f32[3,128,128]{2,1,0:T(8,128)}, f32[3,128,128]{2,1,0:T(8,128)}), (f32[3,128,128]{2,1,0:T(8,128)}, f32[3,128,128]{2,1,0:T(8,128)}, f32[3,128,128]{2,1,0:T(8,128)}, ...) | async-done | bytes 786448 | tf_op jit(solution)/shard_map/psum | solution.py:86
  407.9 5.2 fusion.82
  456.0 6.6 fusion.86
  462.7 11.7 %fusion.83 = (f32[3,64,128]{2,1,0:T(8,128)S(1)}, f32[3,32,128]{2,1,0:T(8,128)S(1)}, f32[3,32,64,128]{3,2,1,0:T(8,128)}) fusion(f32[3,64,128]{2,1,0:T(8,128)S(1)} %copy-done.51, f32[3,32,128]{2,1,0:T(8,128)S(1)} %copy-done.57, f32[3,32,64,128]{3,2,1,0:T(8,128)S(1)} %bitcast.150, f32[128]{0:T(128)S(1)} %copy-done.60, ...), kind=kOutput, calls=%fused_computation.312 | convolution fusion | flops 1822126080 | bytes 21037568 | tf_op jit(solution)/shard_map/dot_general | solution.py:32
  488.8 30.1 %all-reduce.29.cloned.1.call-done = (f32[3,128,128]{2,1,0:T(8,128)}, f32[3,128,128]{2,1,0:T(8,128)}, f32[3,128,128]{2,1,0:T(8,128)}, f32[3,128,128]{2,1,0:T(8,128)}) async-done(((f32[3,128,128]{2,1,0:T(8,128)}, f32[3,128,128]{2,1,0:T(8,128)}, f32[3,128,128]{2,1,0:T(8,128)}, f32[3,128,128]{2,1,0:T(8,128)}), (f32[3,128,128]{2,1,0:T(8,128)}, f32[3,128,128]{2,1,0:T(8,128)}, f32[3,128,128]{2,1,0:T(8,128)}, ...) | async-done | bytes 786448 | tf_op jit(solution)/shard_map/psum | solution.py:86
  522.8 33.6 %all-reduce.21.cloned.1.call-done = (f32[3,128,128]{2,1,0:T(8,128)}, f32[3,128,128]{2,1,0:T(8,128)}, f32[3,128,128]{2,1,0:T(8,128)}, f32[3,128,128]{2,1,0:T(8,128)}) async-done(((f32[3,128,128]{2,1,0:T(8,128)}, f32[3,128,128]{2,1,0:T(8,128)}, f32[3,128,128]{2,1,0:T(8,128)}, f32[3,128,128]{2,1,0:T(8,128)}), (f32[3,128,128]{2,1,0:T(8,128)}, f32[3,128,128]{2,1,0:T(8,128)}, f32[3,128,128]{2,1,0:T(8,128)}, ...) | async-done | bytes 786448 | tf_op jit(solution)/shard_map/psum | solution.py:86
  560.1 7.8 fusion.79
  580.7 7.8 convolution_convert_fusion
  609.7 5.0 copy-done.59
  614.7 7.3 convolution_bitcast_fusion.3
  622.1 7.6 convolution_bitcast_fusion.2
  638.9 26.6 %reduce-scatter.3.cloned.1.call-done = bf16[256,2048]{1,0:T(8,128)(2,1)} async-done(((bf16[1024,2048]{1,0:T(8,128)(2,1)}), bf16[256,2048]{1,0:T(8,128)(2,1)}) %reduce-scatter.3.cloned.1.call-update) | async-done | bytes 1048592 | tf_op jit(solution)/shard_map/reduce_scatter | solution.py:175
  668.3 41.1 %all-reduce = (f32[128]{0:T(128)}, f32[2,128]{1,0:T(2,128)}) all-reduce(f32[128]{0:T(128)S(1)} %add.392, f32[2,128]{1,0:T(2,128)S(1)} %maximum_add_fusion.1), channel_id=1, replica_groups=mesh['obj'=4,'plane'=4,'tile'=2] {'obj','plane','tile'}, use_global_device_ids=true, to_apply=%region_52.53 | all-reduce | flops 384 | bytes 3072 | tf_op jit(solution)/shard_map/psum | solution.py:184
  716.7 87.3 %all-reduce.19.cloned.1.call-done = f32[2,1152,128]{2,1,0:T(8,128)} async-done(((f32[2,1152,128]{2,1,0:T(8,128)}), f32[2,1152,128]{2,1,0:T(8,128)}) %all-reduce.19.cloned.1.call-update) | async-done | bytes 1179664 | tf_op jit(solution)/shard_map/psum | solution.py:184
  804.0 43.9 %reduce-scatter.5.cloned.1.call-done = f32[32,2048]{1,0:T(8,128)} async-done(((f32[256,2048]{1,0:T(8,128)}), f32[32,2048]{1,0:T(8,128)}) %reduce-scatter.5.cloned.1.call-update) | async-done | bytes 262160 | tf_op jit(solution)/shard_map/reduce_scatter | solution.py:183
  (424 shorter events, 288.5 us)
Async XLA Ops:
  7.2 102.6 %all-reduce.35.cloned.1.call-start = ((), (), s32[]{:S(2)}) async-start(), calls=%async_computation.12 | async-start | bytes 1572864 | tf_op jit(solution)/shard_map/psum | solution.py:86
  13.0 63.4 %collective-permute-start = (bf16[3,1,64,128]{3,2,1,0:T(8,128)(2,1)}, bf16[3,1,64,128]{3,2,1,0:T(8,128)(2,1)}, u32[]{:S(2)}, u32[]{:S(2)}) collective-permute-start(bf16[3,1,64,128]{3,2,1,0:T(8,128)(2,1)} %get-tuple-element.117), channel_id=1, source_target_pairs={{0,2},{2,4},{4,6},{1,3},{3,5},{5,7},{8,10},{10,12},{12,14},{9,11},... | collective-permute-start | bytes 147464 | tf_op jit(solution)/shard_map/ppermute | solution.py:14
  16.0 60.4 %collective-permute-start.1 = (bf16[3,1,64,128]{3,2,1,0:T(8,128)(2,1)}, bf16[3,1,64,128]{3,2,1,0:T(8,128)(2,1)}, u32[]{:S(2)}, u32[]{:S(2)}) collective-permute-start(bf16[3,1,64,128]{3,2,1,0:T(8,128)(2,1)} %get-tuple-element.118), channel_id=1, source_target_pairs={{2,0},{4,2},{6,4},{3,1},{5,3},{7,5},{10,8},{12,10},{14,12},{11,9},... | collective-permute-start | bytes 147464 | tf_op jit(solution)/shard_map/ppermute | solution.py:15
  18.0 52.9 %collective-permute-start.12 = (bf16[3,1,64,128]{3,2,1,0:T(8,128)(2,1)}, bf16[3,1,64,128]{3,2,1,0:T(8,128)(2,1)}, u32[]{:S(2)}, u32[]{:S(2)}) collective-permute-start(bf16[3,1,64,128]{3,2,1,0:T(8,128)(2,1)} %get-tuple-element.121), channel_id=1, source_target_pairs={{0,2},{2,4},{4,6},{1,3},{3,5},{5,7},{8,10},{10,12},{12,14},{9,11},... | collective-permute-start | bytes 147464 | tf_op jit(solution)/shard_map/ppermute | solution.py:14
  23.1 47.8 %collective-permute-start.13 = (bf16[3,1,64,128]{3,2,1,0:T(8,128)(2,1)}, bf16[3,1,64,128]{3,2,1,0:T(8,128)(2,1)}, u32[]{:S(2)}, u32[]{:S(2)}) collective-permute-start(bf16[3,1,64,128]{3,2,1,0:T(8,128)(2,1)} %get-tuple-element.122), channel_id=1, source_target_pairs={{2,0},{4,2},{6,4},{3,1},{5,3},{7,5},{10,8},{12,10},{14,12},{11,9},... | collective-permute-start | bytes 147464 | tf_op jit(solution)/shard_map/ppermute | solution.py:15
  55.0 94.2 %all-reduce.27.cloned.1.call-start = ((), (), s32[]{:S(2)}) async-start(), calls=%async_computation.8 | async-start | bytes 1572864 | tf_op jit(solution)/shard_map/psum | solution.py:86
  71.7 11.8 %collective-permute-start.15 = (bf16[3,34,1,128]{3,2,1,0:T(2,128)(2,1)S(1)}, bf16[3,34,1,128]{3,2,1,0:T(2,128)(2,1)S(1)}, u32[]{:S(2)}, u32[]{:S(2)}) collective-permute-start(bf16[3,34,1,128]{3,2,1,0:T(2,128)(2,1)S(1)} %get-tuple-element.101), channel_id=1, source_target_pairs={{0,1},{2,3},{4,5},{6,7},{8,9},{10,11},{12,13},{14,15},{16,17},{18,... | collective-permute-start | bytes 78344 | tf_op jit(solution)/shard_map/ppermute | solution.py:14
  77.2 12.9 %collective-permute-start.3 = (bf16[3,34,1,128]{3,2,1,0:T(2,128)(2,1)S(1)}, bf16[3,34,1,128]{3,2,1,0:T(2,128)(2,1)S(1)}, u32[]{:S(2)}, u32[]{:S(2)}) collective-permute-start(bf16[3,34,1,128]{3,2,1,0:T(2,128)(2,1)S(1)} %get-tuple-element.93), channel_id=1, source_target_pairs={{0,1},{2,3},{4,5},{6,7},{8,9},{10,11},{12,13},{14,15},{16,17},{18,... | collective-permute-start | bytes 78344 | tf_op jit(solution)/shard_map/ppermute | solution.py:14
  109.8 151.2 %all-reduce.33.cloned.1.call-start = ((), (), s32[]{:S(2)}) async-start(), calls=%async_computation.11 | async-start | bytes 1572864 | tf_op jit(solution)/shard_map/psum | solution.py:86
  159.4 11.0 %collective-permute-start.4 = (bf16[3,1,64,128]{3,2,1,0:T(8,128)(2,1)S(1)}, bf16[3,1,64,128]{3,2,1,0:T(8,128)(2,1)S(1)}, u32[]{:S(2)}, u32[]{:S(2)}) collective-permute-start(bf16[3,1,64,128]{3,2,1,0:T(8,128)(2,1)S(1)} %get-tuple-element.119), channel_id=1, source_target_pairs={{0,2},{2,4},{4,6},{1,3},{3,5},{5,7},{8,10},{10,12},{12,14},{9,11},... | collective-permute-start | bytes 147464 | tf_op jit(solution)/shard_map/ppermute | solution.py:14
  164.6 12.0 %collective-permute-start.19 = (bf16[3,34,1,128]{3,2,1,0:T(2,128)(2,1)S(1)}, bf16[3,34,1,128]{3,2,1,0:T(2,128)(2,1)S(1)}, u32[]{:S(2)}, u32[]{:S(2)}) collective-permute-start(bf16[3,34,1,128]{3,2,1,0:T(2,128)(2,1)S(1)} %get-tuple-element.105), channel_id=1, source_target_pairs={{1,0},{3,2},{5,4},{7,6},{9,8},{11,10},{13,12},{15,14},{17,16},{19,... | collective-permute-start | bytes 78344 | tf_op jit(solution)/shard_map/ppermute | solution.py:15
  165.9 10.7 %collective-permute-start.18 = (bf16[3,34,1,128]{3,2,1,0:T(2,128)(2,1)S(1)}, bf16[3,34,1,128]{3,2,1,0:T(2,128)(2,1)S(1)}, u32[]{:S(2)}, u32[]{:S(2)}) collective-permute-start(bf16[3,34,1,128]{3,2,1,0:T(2,128)(2,1)S(1)} %get-tuple-element.106), channel_id=1, source_target_pairs={{0,1},{2,3},{4,5},{6,7},{8,9},{10,11},{12,13},{14,15},{16,17},{18,... | collective-permute-start | bytes 78344 | tf_op jit(solution)/shard_map/ppermute | solution.py:14
  170.6 13.7 %collective-permute-start.7 = (bf16[3,34,1,128]{3,2,1,0:T(2,128)(2,1)S(1)}, bf16[3,34,1,128]{3,2,1,0:T(2,128)(2,1)S(1)}, u32[]{:S(2)}, u32[]{:S(2)}) collective-permute-start(bf16[3,34,1,128]{3,2,1,0:T(2,128)(2,1)S(1)} %get-tuple-element.97), channel_id=1, source_target_pairs={{1,0},{3,2},{5,4},{7,6},{9,8},{11,10},{13,12},{15,14},{17,16},{19,... | collective-permute-start | bytes 78344 | tf_op jit(solution)/shard_map/ppermute | solution.py:15
  171.9 12.4 %collective-permute-start.6 = (bf16[3,34,1,128]{3,2,1,0:T(2,128)(2,1)S(1)}, bf16[3,34,1,128]{3,2,1,0:T(2,128)(2,1)S(1)}, u32[]{:S(2)}, u32[]{:S(2)}) collective-permute-start(bf16[3,34,1,128]{3,2,1,0:T(2,128)(2,1)S(1)} %get-tuple-element.98), channel_id=1, source_target_pairs={{0,1},{2,3},{4,5},{6,7},{8,9},{10,11},{12,13},{14,15},{16,17},{18,... | collective-permute-start | bytes 78344 | tf_op jit(solution)/shard_map/ppermute | solution.py:14
  223.8 74.6 %all-reduce.25.cloned.1.call-start = ((), (), s32[]{:S(2)}) async-start(), calls=%async_computation.7 | async-start | bytes 1572864 | tf_op jit(solution)/shard_map/psum | solution.py:86
  261.0 105.7 %all-reduce.31.cloned.1.call-start = ((), (), s32[]{:S(2)}) async-start(), calls=%async_computation.10 | async-start | bytes 1572864 | tf_op jit(solution)/shard_map/psum | solution.py:86
  306.1 30.4 %collective-permute-start.24 = (bf16[3,1,64,128]{3,2,1,0:T(8,128)(2,1)}, bf16[3,1,64,128]{3,2,1,0:T(8,128)(2,1)}, u32[]{:S(2)}, u32[]{:S(2)}) collective-permute-start(bf16[3,1,64,128]{3,2,1,0:T(8,128)(2,1)} %get-tuple-element.109), channel_id=1, source_target_pairs={{0,2},{2,4},{4,6},{1,3},{3,5},{5,7},{8,10},{10,12},{12,14},{9,11},... | collective-permute-start | bytes 147464 | tf_op jit(solution)/shard_map/ppermute | solution.py:14
  308.0 28.5 %collective-permute-start.25 = (bf16[3,1,64,128]{3,2,1,0:T(8,128)(2,1)}, bf16[3,1,64,128]{3,2,1,0:T(8,128)(2,1)}, u32[]{:S(2)}, u32[]{:S(2)}) collective-permute-start(bf16[3,1,64,128]{3,2,1,0:T(8,128)(2,1)} %get-tuple-element.110), channel_id=1, source_target_pairs={{2,0},{4,2},{6,4},{3,1},{5,3},{7,5},{10,8},{12,10},{14,12},{11,9},... | collective-permute-start | bytes 147464 | tf_op jit(solution)/shard_map/ppermute | solution.py:15
  328.6 75.5 %all-reduce.23.cloned.1.call-start = ((), (), s32[]{:S(2)}) async-start(), calls=%async_computation.6 | async-start | bytes 1572864 | tf_op jit(solution)/shard_map/psum | solution.py:86
  332.1 34.8 %collective-permute-start.28 = (bf16[3,1,64,128]{3,2,1,0:T(8,128)(2,1)}, bf16[3,1,64,128]{3,2,1,0:T(8,128)(2,1)S(1)}, u32[]{:S(2)}, u32[]{:S(2)}) collective-permute-start(bf16[3,1,64,128]{3,2,1,0:T(8,128)(2,1)} %get-tuple-element.107), channel_id=1, source_target_pairs={{0,2},{2,4},{4,6},{1,3},{3,5},{5,7},{8,10},{10,12},{12,14},{9,11},... | collective-permute-start | bytes 147464 | tf_op jit(solution)/shard_map/ppermute | solution.py:14
  335.2 31.7 %collective-permute-start.29 = (bf16[3,1,64,128]{3,2,1,0:T(8,128)(2,1)}, bf16[3,1,64,128]{3,2,1,0:T(8,128)(2,1)S(1)}, u32[]{:S(2)}, u32[]{:S(2)}) collective-permute-start(bf16[3,1,64,128]{3,2,1,0:T(8,128)(2,1)} %get-tuple-element.108), channel_id=1, source_target_pairs={{2,0},{4,2},{6,4},{3,1},{5,3},{7,5},{10,8},{12,10},{14,12},{11,9},... | collective-permute-start | bytes 147464 | tf_op jit(solution)/shard_map/ppermute | solution.py:15
  338.0 36.8 %collective-permute-start.27 = (bf16[3,34,1,128]{3,2,1,0:T(2,128)(2,1)}, bf16[3,34,1,128]{3,2,1,0:T(2,128)(2,1)S(1)}, u32[]{:S(2)}, u32[]{:S(2)}) collective-permute-start(bf16[3,34,1,128]{3,2,1,0:T(2,128)(2,1)} %get-tuple-element.81), channel_id=1, source_target_pairs={{1,0},{3,2},{5,4},{7,6},{9,8},{11,10},{13,12},{15,14},{17,16},{19,... | collective-permute-start | bytes 78344 | tf_op jit(solution)/shard_map/ppermute | solution.py:15
  339.3 35.5 %collective-permute-start.26 = (bf16[3,34,1,128]{3,2,1,0:T(2,128)(2,1)}, bf16[3,34,1,128]{3,2,1,0:T(2,128)(2,1)}, u32[]{:S(2)}, u32[]{:S(2)}) collective-permute-start(bf16[3,34,1,128]{3,2,1,0:T(2,128)(2,1)} %get-tuple-element.82), channel_id=1, source_target_pairs={{0,1},{2,3},{4,5},{6,7},{8,9},{10,11},{12,13},{14,15},{16,17},{18,... | collective-permute-start | bytes 78344 | tf_op jit(solution)/shard_map/ppermute | solution.py:14
  366.7 152.1 %all-reduce.29.cloned.1.call-start = ((), (), s32[]{:S(2)}) async-start(), calls=%async_computation.9 | async-start | bytes 1572864 | tf_op jit(solution)/shard_map/psum | solution.py:86
  367.7 229.5 %collective-permute-start.31 = (bf16[3,34,1,128]{3,2,1,0:T(2,128)(2,1)}, bf16[3,34,1,128]{3,2,1,0:T(2,128)(2,1)}, u32[]{:S(2)}, u32[]{:S(2)}) collective-permute-start(bf16[3,34,1,128]{3,2,1,0:T(2,128)(2,1)} %get-tuple-element.77), channel_id=1, source_target_pairs={{1,0},{3,2},{5,4},{7,6},{9,8},{11,10},{13,12},{15,14},{17,16},{19,... | collective-permute-start | bytes 78344 | tf_op jit(solution)/shard_map/ppermute | solution.py:15
  369.0 228.3 %collective-permute-start.30 = (bf16[3,34,1,128]{3,2,1,0:T(2,128)(2,1)}, bf16[3,34,1,128]{3,2,1,0:T(2,128)(2,1)}, u32[]{:S(2)}, u32[]{:S(2)}) collective-permute-start(bf16[3,34,1,128]{3,2,1,0:T(2,128)(2,1)} %get-tuple-element.78), channel_id=1, source_target_pairs={{0,1},{2,3},{4,5},{6,7},{8,9},{10,11},{12,13},{14,15},{16,17},{18,... | collective-permute-start | bytes 78344 | tf_op jit(solution)/shard_map/ppermute | solution.py:14
  420.9 9.4 %collective-permute-start.23 = (bf16[3,34,1,128]{3,2,1,0:T(2,128)(2,1)S(1)}, bf16[3,34,1,128]{3,2,1,0:T(2,128)(2,1)S(1)}, u32[]{:S(2)}, u32[]{:S(2)}) collective-permute-start(bf16[3,34,1,128]{3,2,1,0:T(2,128)(2,1)S(1)} %get-tuple-element.89), channel_id=1, source_target_pairs={{0,1},{2,3},{4,5},{6,7},{8,9},{10,11},{12,13},{14,15},{16,17},{18,... | collective-permute-start | bytes 78344 | tf_op jit(solution)/shard_map/ppermute | solution.py:14
  425.8 13.4 %collective-permute-start.11 = (bf16[3,34,1,128]{3,2,1,0:T(2,128)(2,1)S(1)}, bf16[3,34,1,128]{3,2,1,0:T(2,128)(2,1)S(1)}, u32[]{:S(2)}, u32[]{:S(2)}) collective-permute-start(bf16[3,34,1,128]{3,2,1,0:T(2,128)(2,1)S(1)} %get-tuple-element.85), channel_id=1, source_target_pairs={{0,1},{2,3},{4,5},{6,7},{8,9},{10,11},{12,13},{14,15},{16,17},{18,... | collective-permute-start | bytes 78344 | tf_op jit(solution)/shard_map/ppermute | solution.py:14
  479.7 76.7 %all-reduce.21.cloned.1.call-start = ((), (), s32[]{:S(2)}) async-start(), calls=%async_computation.5 | async-start | bytes 1572864 | tf_op jit(solution)/shard_map/psum | solution.py:86
  518.8 146.7 %reduce-scatter.3.cloned.1.call-start = ((), (), s32[]{:S(2)}) async-start(), calls=%async_computation.2 | async-start | bytes 5242880 | tf_op jit(solution)/shard_map/reduce_scatter | solution.py:175
  588.6 215.4 %all-reduce.19.cloned.1.call-start = ((), (), s32[]{:S(2)}) async-start(), calls=%async_computation.4 | async-start | bytes 2359296 | tf_op jit(solution)/shard_map/psum | solution.py:184
  638.8 209.1 %reduce-scatter.5.cloned.1.call-start = ((), (), s32[]{:S(2)}) async-start(), calls=%async_computation.3 | async-start | bytes 2359296 | tf_op jit(solution)/shard_map/reduce_scatter | solution.py:183
  (85 other events, 720.1 us)
Sparse Core Ops, SparseCore 0:
  55.2 38.6 all-reduce.34
  109.9 39.2 all-reduce.26
  223.9 36.9 all-reduce.32
  263.4 34.9 all-reduce.24
  328.7 37.9 all-reduce.30
  369.1 34.9 all-reduce.22
  479.8 38.9 all-reduce.28
  521.4 34.9 all-reduce.20
  588.7 76.7 reduce-scatter.2
  671.3 132.6 all-reduce.18
  807.9 40.0 reduce-scatter.4
